TPU v7x, 256 devices: a whole 4x4x8 slice. The times are simulated.
256 devices in a mesh: row: 8 (over x, y_lo), col: 32 (over y_hi, z, core).
Axes of the slice: x: 4, y: 4 (y_hi: 2, y_lo: 2; y = y_hi * 2 + y_lo), z: 8, core: 2. Of those that a mesh axis runs over, the one named last changes fastest.
Arguments:
- features: bfloat16 [65536, 128], P(('row', 'col')), may hold values from -6 to 6
- degrees: int32 [65536], P(('row', 'col')), may hold values from 32 to 159
- adj_tiles: bfloat16 [8, 32, 256, 4096], P('row', 'col'), may hold values from 0 to 0.22472483, as said below
- tile_rows: int32 [8, 32, 256], P('row', 'col'), may hold values from 0 to 127
- tile_cols: int32 [8, 32, 256], P('row', 'col'), may hold values from 0 to 31
- tile_counts: int32 [8, 32], P('row', 'col'), may hold values from 64 to 256, as said below
Outputs:
- propagated: bfloat16 [65536, 128], P(('row', 'col'))
Inputs may be any that keep to these rules, and one draw needn't show every extreme that they name: Each block holds at most 256 live tiles, in its first tile_counts slots; some block holds exactly 256. `adj_tiles`: edge weights are zero or positive.
All inputs are finite; a program needn't handle non-finite values.
Results may differ from a plain program's by a relative error of at most 0.0054.
Values may be sent and summed in bfloat16 or wider, within the bound.
A program may use at most 128 MiB of HBM per device.

v0:
```python
import jax
import jax.numpy as jnp
from jax import lax
from jax.sharding import PartitionSpec as P

TILE = 64
KNN = 32
STEPS = 2
ALPHA = 0.1


def shards(features, degrees, adj_tiles, tile_rows, tile_cols, tile_counts):
    col_count = lax.axis_size("col")
    nodes_dev = features.shape[0]
    feat_width = features.shape[1]
    tile_slots = adj_tiles.shape[2]
    dev_tiles = adj_tiles.reshape(tile_slots, TILE, TILE)
    row_ids_all = tile_rows.reshape(tile_slots)
    col_ids_all = tile_cols.reshape(tile_slots)
    live_count = tile_counts.reshape(())
    block_len = min(256, tile_slots)
    num_turns = tile_slots // block_len
    row_tiles = nodes_dev * col_count // TILE
    norm_scale = jnp.sqrt(KNN / degrees.astype(jnp.float32))[:, None]
    teleport = ALPHA * features.astype(jnp.float32)
    current = features.astype(jnp.float32)
    for repeat in range(STEPS):
        source = (norm_scale * current).astype(jnp.bfloat16)
        col_panel = lax.all_gather(source, "row", axis=0, tiled=True).reshape(-1, TILE, feat_width)

        def add_block(turn_index, totals):
            first_tile = turn_index * block_len
            live_mask = first_tile + jnp.arange(block_len, dtype=jnp.int32) < live_count
            inputs = col_panel[col_ids_all]
            products = jnp.einsum(
                "tab,tbf->taf", dev_tiles, inputs, preferred_element_type=jnp.float32
            )
            products = jnp.where(live_mask[:, None, None], products, jnp.zeros_like(products))
            return totals.at[row_ids_all].add(products)

        start_tot = jnp.zeros((row_tiles, TILE, feat_width), jnp.float32)
        totals = lax.fori_loop(0, num_turns, add_block, start_tot)
        partial_rows = totals.reshape(row_tiles * TILE, feat_width)
        summed = lax.psum(partial_rows, "col")
        own_rows = lax.dynamic_slice_in_dim(summed, lax.axis_index("col") * nodes_dev, nodes_dev, 0)
        current = (1.0 - ALPHA) * norm_scale * own_rows + teleport
    return current.astype(jnp.bfloat16)


def solution(mesh):
    return jax.shard_map(
        shards,
        mesh=mesh,
        in_specs=(
            P(("row", "col"), None),
            P(("row", "col")),
            P("row", "col", None, None),
            P("row", "col", None),
            P("row", "col", None),
            P("row", "col"),
        ),
        out_specs=P(("row", "col"), None),
        check_vma=False,
    )
```

profile of v0, /device:TPU:1, one launch (start us, length us, event | category | flops | bytes accessed | tf_op | source)
XLA Modules:
  0.0 748.5 jit_solution(6147863713044268704)
XLA Ops:
  6.5 0.0 all-reduce.3.cloned.1.call-start
  7.2 0.7 compare_select_fusion.1
  7.9 0.7 compare_select_fusion
  8.6 0.7 broadcast_multiply_fusion
  9.3 0.9 fusion.5
  10.2 24.6 %all_gather.6 = bf16[2048,128]{1,0:T(8,128)(2,1)S(1)} all-gather(bf16[256,128]{1,0:T(8,128)(2,1)S(1)} %fusion.5), channel_id=1, replica_groups=mesh['row'=8,'col'=32] {'row'}, dimensions={0}, use_global_device_ids=true | all-gather | bytes 589824 | tf_op jit(solution)/shard_map/all_gather | solution.py:29
  34.8 3.3 copy.7
  38.1 6.6 copy.8
  44.8 3.0 gather_fusion
  47.8 7.9 %select_bitcast_fusion.1 = f32[256,64,128]{2,1,0:T(8,128)} fusion(pred[256]{0:T(512)(128)(4,1)S(1)} %iota_compare_fusion, bf16[256,64,64]{2,1,0:T(8,128)(2,1)} %copy.8, bf16[256,64,128]{2,1,0:T(8,128)(2,1)} %gather_fusion), kind=kOutput, calls=%fused_computation.5 | convolution fusion | flops 270532608 | bytes 14680320 | tf_op jit(solution)/shard_map/while/body/eval_jaxpr/tab,tbf->taf/dot_general | solution.py:35
  55.7 2.5 broadcast.71.clone
  58.2 39.4 %scatter_fusion = f32[128,64,128]{2,1,0:T(8,128)} fusion(f32[128,64,128]{2,1,0:T(8,128)} %broadcast.71.clone, s32[256]{0:T(256)S(1)} %bitcast.26, f32[256,64,128]{2,1,0:T(8,128)} %select_bitcast_fusion.1), kind=kCustom, calls=%fused_computation.2 | custom fusion | flops 2097152 | bytes 25166848 | tf_op jit(solution)/shard_map/while/body/eval_jaxpr/scatter-add | solution.py:39
  97.6 0.0 copy-start
  97.6 0.0 all-reduce.3.cloned.1.call-update
  97.6 0.0 all-reduce.5.cloned.1.call-start
  97.7 286.3 %all-reduce.3.cloned.1.call-done = f32[8192,128]{1,0:T(8,128)} async-done(((f32[8192,128]{1,0:T(8,128)}), f32[8192,128]{1,0:T(8,128)}) %all-reduce.3.cloned.1.call-update) | async-done | bytes 4194320 | tf_op jit(solution)/shard_map/psum | solution.py:44
  384.0 0.0 copy-done
  384.0 1.0 fusion.3
  385.0 23.4 %all_gather.7 = bf16[2048,128]{1,0:T(8,128)(2,1)S(1)} all-gather(bf16[256,128]{1,0:T(8,128)(2,1)S(1)} %fusion.3), channel_id=1, replica_groups=mesh['row'=8,'col'=32] {'row'}, dimensions={0}, use_global_device_ids=true | all-gather | bytes 589824 | tf_op jit(solution)/shard_map/all_gather | solution.py:29
  408.4 3.1 gather_fusion.1
  411.5 7.9 %select_bitcast_fusion = f32[256,64,128]{2,1,0:T(8,128)} fusion(pred[256]{0:T(512)(128)(4,1)S(1)} %iota_compare_fusion, bf16[256,64,64]{2,1,0:T(8,128)(2,1)} %copy.8, bf16[256,64,128]{2,1,0:T(8,128)(2,1)} %gather_fusion.1), kind=kOutput, calls=%fused_computation.4 | convolution fusion | flops 270532608 | bytes 14680320 | tf_op jit(solution)/shard_map/while/body/eval_jaxpr/tab,tbf->taf/dot_general | solution.py:35
  419.4 2.5 broadcast.71
  421.9 39.3 %scatter_fusion.1 = f32[128,64,128]{2,1,0:T(8,128)} fusion(f32[128,64,128]{2,1,0:T(8,128)} %broadcast.71, s32[256]{0:T(256)S(1)} %bitcast.27, f32[256,64,128]{2,1,0:T(8,128)} %select_bitcast_fusion), kind=kCustom, calls=%fused_computation.3 | custom fusion | flops 2097152 | bytes 25166848 | tf_op jit(solution)/shard_map/while/body/eval_jaxpr/scatter-add | solution.py:39
  461.2 0.0 all-reduce.5.cloned.1.call-update
  461.3 278.8 %all-reduce.5.cloned.1.call-done = f32[8192,128]{1,0:T(8,128)} async-done(((f32[8192,128]{1,0:T(8,128)}), f32[8192,128]{1,0:T(8,128)}) %all-reduce.5.cloned.1.call-update) | async-done | bytes 4194320 | tf_op jit(solution)/shard_map/psum | solution.py:44
  740.1 1.6 fusion.4
  (2 shorter events, 0.0 us)
Async XLA Ops:
  6.5 377.4 %all-reduce.3.cloned.1.call-start = ((), (), s32[]{:S(2)}) async-start(), calls=%async_computation | async-start | bytes 8388608 | tf_op jit(solution)/shard_map/psum | solution.py:44
  97.6 286.3 %copy-start = (bf16[256,128]{1,0:T(8,128)(2,1)S(1)}, bf16[256,128]{1,0:T(8,128)(2,1)}, u32[]{:S(2)}) copy-start(bf16[256,128]{1,0:T(8,128)(2,1)} %param.6) | copy-start | bytes 196612
  97.6 642.4 %all-reduce.5.cloned.1.call-start = ((), (), s32[]{:S(2)}) async-start(), calls=%async_computation.1 | async-start | bytes 8388608 | tf_op jit(solution)/shard_map/psum | solution.py:44
Sparse Core Ops, SparseCore 0:
  97.8 286.1 all-reduce.2
  461.4 278.6 all-reduce.4
where the time goes:
time: 750 us; the launch traced here: 749 us
  waiting for transfers between devices  565 us (75%)
  other arithmetic  84.4 us (11%)
  blocking collectives  48.1 us (6%)
  local copies, waits for them, and re-layouts  21 us (3%)
  matrix products  15.9 us (2%)
  between operations  14.1 us (2%)
    psum x2, waiting for transfers between devices, shards(): summed = lax.psum(partial_rows, 'col')  565 us
    scatter-add x2, other arithmetic, add_block(): return totals.at[row_ids_all].add(products)  78.7 us
    all_gather x2, blocking collectives, shards(): lax.all_gather(source, 'row', axis=0, tiled=True)  48.1 us
    dot_general x2, matrix products, add_block(): jnp.einsum('tab,tbf->taf', dev_tiles, inputs, preferred_element_type=jnp....  15.9 us
  transfers between devices with their start and end apart: 2, of which 2 were waited for; matrix products, arithmetic and copies ran while one was open for 0% of the time, Pallas kernels for 0%

commit v1 on v0

--- a/solution.py
+++ b/solution.py
@@ -1,3 +1,4 @@
+import functools
 import jax
 import jax.numpy as jnp
 from jax import lax
@@ -7,6 +8,18 @@
 KNN = 32
 STEPS = 2
 ALPHA = 0.1
+
+
+def pipes_map(array_in, named_axis):
+    return jnp.concatenate(
+        jax.lax.all_to_all(
+            jnp.stack(jax.lax.axis_size(named_axis) * [array_in], axis=0), named_axis, 0, 0
+        ),
+        0,
+    )
+
+
+deliver_view = functools.partial(pipes_map, named_axis="row")
 
 
 def shards(features, degrees, adj_tiles, tile_rows, tile_cols, tile_counts):
@@ -26,7 +39,7 @@
     current = features.astype(jnp.float32)
     for repeat in range(STEPS):
         source = (norm_scale * current).astype(jnp.bfloat16)
-        col_panel = lax.all_gather(source, "row", axis=0, tiled=True).reshape(-1, TILE, feat_width)
+        col_panel = deliver_view(source).reshape(-1, TILE, feat_width)
 
         def add_block(turn_index, totals):
             first_tile = turn_index * block_len

time: 750 us -> 711 us (0.948)
  blocking collectives: 48.1 us -> 12.4 us
  waiting for transfers between devices: 565 us -> 556 us
    all_gather x2 -> x0, blocking collectives: 48.1 us -> none  [shards(): lax.all_gather(source, 'row', axis=0, tiled=True)]
    all_to_all x0 -> x1, blocking collectives: none -> 12.4 us  [pipes_map(): jax.lax.all_to_all(jnp.stack(jax.lax.axis_size(named_axis) * [array_in],...]
    psum x2, waiting for transfers between devices: 565 us -> 556 us  [shards(): summed = lax.psum(partial_rows, 'col')]
  transfers between devices with their start and end apart: 2 -> 3, of which waited for: 2 -> 2; matrix products, arithmetic and copies ran while one was open for 0% -> 1% of each run, Pallas kernels for 0% -> 0%
where the time goes in v1:
time: 711 us; the launch traced here: 710 us
  waiting for transfers between devices  556 us (78%)
  other arithmetic  83.7 us (12%)
  local copies, waits for them, and re-layouts  21.9 us (3%)
  matrix products  15.9 us (2%)
  between operations  14.1 us (2%)
  blocking collectives  12.4 us (2%)
    psum x2, waiting for transfers between devices, shards(): summed = lax.psum(partial_rows, 'col')  556 us
    scatter-add x2, other arithmetic, add_block(): return totals.at[row_ids_all].add(products)  78.7 us
    dot_general x2, matrix products, add_block(): jnp.einsum('tab,tbf->taf', dev_tiles, inputs, preferred_element_type=jnp....  15.9 us
  transfers between devices with their start and end apart: 3, of which 2 were waited for; matrix products, arithmetic and copies ran while one was open for 1% of the time, Pallas kernels for 0%

profile of v1, /device:TPU:1, one launch (start us, length us, event | category | flops | bytes accessed | tf_op | source)
XLA Modules:
  0.0 710.3 jit_solution(12768226916152396711)
XLA Ops:
  6.5 0.7 broadcast_multiply_fusion
  7.2 0.9 fusion.5
  8.2 0.9 stack.4
  9.0 5.9 all-to-all-start
  14.9 0.0 all-reduce.3.cloned.1.call-start
  14.9 0.7 compare_select_fusion
  16.3 3.3 copy.7
  19.6 0.0 copy-start.1
  19.6 6.6 copy.8
  26.2 0.0 copy-done.1
  26.2 0.0 all-to-all-done
  26.3 3.1 gather_fusion
  29.3 7.9 %select_bitcast_fusion.1 = f32[256,64,128]{2,1,0:T(8,128)} fusion(pred[256]{0:T(512)(128)(4,1)S(1)} %iota_compare_fusion, bf16[256,64,64]{2,1,0:T(8,128)(2,1)} %copy.8, bf16[256,64,128]{2,1,0:T(8,128)(2,1)} %gather_fusion), kind=kOutput, calls=%fused_computation.5 | convolution fusion | flops 270532608 | bytes 14680320 | tf_op jit(solution)/shard_map/while/body/eval_jaxpr/tab,tbf->taf/dot_general | solution.py:48
  37.2 2.5 broadcast.75.clone
  39.7 39.4 %scatter_fusion = f32[128,64,128]{2,1,0:T(8,128)} fusion(f32[128,64,128]{2,1,0:T(8,128)} %broadcast.75.clone, s32[256]{0:T(256)S(1)} %bitcast.26, f32[256,64,128]{2,1,0:T(8,128)} %select_bitcast_fusion.1), kind=kCustom, calls=%fused_computation.2 | custom fusion | flops 2097152 | bytes 25166848 | tf_op jit(solution)/shard_map/while/body/eval_jaxpr/scatter-add | solution.py:52
  79.1 0.0 copy-start
  79.1 0.0 all-reduce.3.cloned.1.call-update
  79.1 0.0 all-reduce.5.cloned.1.call-start
  79.2 281.8 %all-reduce.3.cloned.1.call-done = f32[8192,128]{1,0:T(8,128)} async-done(((f32[8192,128]{1,0:T(8,128)}), f32[8192,128]{1,0:T(8,128)}) %all-reduce.3.cloned.1.call-update) | async-done | bytes 4194320 | tf_op jit(solution)/shard_map/psum | solution.py:57
  361.0 0.0 copy-done
  361.0 1.0 fusion.3
  362.1 0.1 stack.5
  362.1 12.4 %all_to_all.10 = bf16[8,256,128]{2,1,0:T(8,128)(2,1)S(1)} all-to-all(bf16[8,256,128]{2,1,0:T(8,128)(2,1)S(1)} %stack.5), channel_id=1, replica_groups=mesh['row'=8,'col'=32] {'row'}, dimensions={0} | all-to-all | bytes 1048576 | tf_op jit(solution)/shard_map/all_to_all | solution.py:15
  374.5 3.0 gather_fusion.1
  377.6 7.9 %select_bitcast_fusion = f32[256,64,128]{2,1,0:T(8,128)} fusion(pred[256]{0:T(512)(128)(4,1)S(1)} %iota_compare_fusion, bf16[256,64,64]{2,1,0:T(8,128)(2,1)} %copy.8, bf16[256,64,128]{2,1,0:T(8,128)(2,1)} %gather_fusion.1), kind=kOutput, calls=%fused_computation.4 | convolution fusion | flops 270532608 | bytes 14680320 | tf_op jit(solution)/shard_map/while/body/eval_jaxpr/tab,tbf->taf/dot_general | solution.py:48
  385.5 2.5 broadcast.75
  388.0 39.3 %scatter_fusion.1 = f32[128,64,128]{2,1,0:T(8,128)} fusion(f32[128,64,128]{2,1,0:T(8,128)} %broadcast.75, s32[256]{0:T(256)S(1)} %bitcast.27, f32[256,64,128]{2,1,0:T(8,128)} %select_bitcast_fusion), kind=kCustom, calls=%fused_computation.3 | custom fusion | flops 2097152 | bytes 25166848 | tf_op jit(solution)/shard_map/while/body/eval_jaxpr/scatter-add | solution.py:52
  427.3 0.0 all-reduce.5.cloned.1.call-update
  427.4 274.4 %all-reduce.5.cloned.1.call-done = f32[8192,128]{1,0:T(8,128)} async-done(((f32[8192,128]{1,0:T(8,128)}), f32[8192,128]{1,0:T(8,128)}) %all-reduce.5.cloned.1.call-update) | async-done | bytes 4194320 | tf_op jit(solution)/shard_map/psum | solution.py:57
  701.8 1.6 fusion.4
  (3 shorter events, 0.0 us)
Async XLA Ops:
  9.0 17.2 %all-to-all-start = ((bf16[8,256,128]{2,1,0:T(8,128)(2,1)}), bf16[8,256,128]{2,1,0:T(8,128)(2,1)S(1)}, u32[]{:S(2)}, u32[]{:S(2)}) async-start(bf16[8,256,128]{2,1,0:T(8,128)(2,1)} %stack.4), calls=%async_computation | async-start | bytes 1048576 | tf_op jit(solution)/shard_map/all_to_all | solution.py:15
  14.9 346.1 %all-reduce.3.cloned.1.call-start = ((), (), s32[]{:S(2)}) async-start(), calls=%async_computation.2 | async-start | bytes 8388608 | tf_op jit(solution)/shard_map/psum | solution.py:57
  19.6 6.7 copy-start.1
  79.1 281.9 %copy-start = (bf16[256,128]{1,0:T(8,128)(2,1)S(1)}, bf16[256,128]{1,0:T(8,128)(2,1)}, u32[]{:S(2)}) copy-start(bf16[256,128]{1,0:T(8,128)(2,1)} %param.6) | copy-start | bytes 196612
  79.1 622.7 %all-reduce.5.cloned.1.call-start = ((), (), s32[]{:S(2)}) async-start(), calls=%async_computation.3 | async-start | bytes 8388608 | tf_op jit(solution)/shard_map/psum | solution.py:57
Sparse Core Ops, SparseCore 0:
  79.3 281.7 all-reduce.2
  427.5 274.2 all-reduce.4
